TPU v7x, 32 devices: a whole 2x2x4 slice. The times are simulated.
32 devices in a mesh: blk: 8 (over z, x), rep: 4 (over y, core).
Axes of the slice: x: 2, y: 2, z: 4, core: 2. Of those that a mesh axis runs over, the one named last changes fastest.
Arguments:
- density: bfloat16 [128, 9, 128, 128], P(('blk', 'rep')), may hold values from -0.48 to 0.48, as said below
- pattern: int32 [128, 9], P(('blk', 'rep')), may hold values from 0 to 1, as said below
- orbitals: int32 [128], replicated, may hold values from 96 to 128
Outputs:
- purified: bfloat16 [128, 9, 128, 128], P(('blk', 'rep'))
Inputs may be any that keep to these rules, and one draw needn't show every extreme that they name: `density`: the stored matrix is symmetric: the block at [c, s] is the transpose of the block at [(c + s - 4) mod 128, 8 - s]. The pattern is symmetric: pattern[c, s] = pattern[(c + s - 4) mod 128, 8 - s]; every diagonal block (s = 4) is 1.
All inputs are finite; a program needn't handle non-finite values.
Results may differ from a plain program's by a relative error of at most 0.0037.
Values may be sent and summed in bfloat16 or wider, within the bound.
A program may use at most 64 MiB of HBM per device.

v0:
```python
import jax
import jax.numpy as jnp
from jax import lax
from jax.sharding import PartitionSpec as P


def passed_along(array, axis, by):
    count = lax.axis_size(axis)
    return lax.ppermute(array, axis, [(i, (i + by) % count) for i in range(count)])


def column_terms(widened, own, reach_len):
    own_cols, band_len = (own.shape[0], own.shape[1])
    total = jnp.zeros(own.shape, jnp.float32)
    for step_t in range(band_len):
        first_slot = max(0, step_t - reach_len)
        last_slot = min(band_len - 1, step_t + reach_len)
        first_row = first_slot - step_t + reach_len
        slot_count = last_slot - first_slot + 1
        partial_sum = jnp.einsum(
            "jsab,jbc->jsac",
            widened[step_t : step_t + own_cols, first_row : first_row + slot_count],
            own[:, step_t],
            preferred_element_type=jnp.float32,
        )
        total = total.at[:, first_slot : last_slot + 1].add(partial_sum)
    return total


def per_device(density, pattern, orbitals):
    own_cols, band_len, tile_size = (density.shape[0], density.shape[1], density.shape[2])
    reach_len = (band_len - 1) // 2
    all_blocks = orbitals.shape[0]
    first_col = lax.axis_index(("blk", "rep")) * own_cols
    doubled = jnp.concatenate([orbitals, orbitals])
    start_at = (first_col - reach_len + all_blocks) % all_blocks
    near_counts = lax.dynamic_slice_in_dim(doubled, start_at, own_cols + 2 * reach_len)
    row_counts = jnp.stack(
        [near_counts[slot : slot + own_cols] for slot in range(band_len)], axis=1
    )
    col_counts = near_counts[reach_len : reach_len + own_cols]
    lane_ids = jnp.arange(tile_size, dtype=jnp.int32)
    visible = (
        (lane_ids[None, None, :, None] < row_counts[:, :, None, None])
        & (lane_ids[None, None, None, :] < col_counts[:, None, None, None])
        & (pattern[:, :, None, None] == 1)
    )
    masked = jnp.where(visible, density, jnp.zeros_like(density))
    in_pattern = (pattern == 1)[:, :, None, None]
    hop_count = -(-reach_len // own_cols)
    reaches = []
    for distance in range(-hop_count, hop_count + 1):
        low_end = max(0, -distance * own_cols - reach_len)
        high_end = min(own_cols, own_cols + reach_len - distance * own_cols)
        if distance != 0 and low_end < high_end:
            reaches.append((distance, low_end, high_end))

    def widen(values):
        pieces = []
        for distance, low_end, high_end in reaches:
            if (
                distance > 0
                and len(pieces) == 0
                or (
                    distance > 0
                    and pieces[-1] is not values
                    and (not any((piece is values for piece in pieces)))
                )
            ):
                pieces.append(values)
            pieces.append(passed_along(values, ("blk", "rep"), -distance))
        if not any((piece is values for piece in pieces)):
            pieces.append(values)
        return jnp.concatenate(pieces, axis=0)

    square = column_terms(widen(masked), masked, reach_len)
    squared = jnp.where(in_pattern, square, jnp.zeros_like(square)).astype(jnp.bfloat16)
    cube = column_terms(widen(squared), masked, reach_len)
    mixed = 3.0 * square - 2.0 * cube
    return jnp.where(in_pattern, mixed, jnp.zeros_like(mixed)).astype(jnp.bfloat16)


def solution(mesh):
    placed = (P(("blk", "rep"), None, None, None), P(("blk", "rep"), None), P())
    return jax.shard_map(
        per_device,
        mesh=mesh,
        in_specs=placed,
        out_specs=P(("blk", "rep"), None, None, None),
        check_vma=False,
    )
```

profile of v0, /device:TPU:12, one launch (start us, length us, event | category | flops | bytes accessed | tf_op | source)
XLA Modules:
  0.0 83.5 jit_solution(17809338700506609080)
XLA Ops:
  0.0 0.7 broadcast_compare_fusion
  0.7 0.7 pad_add_fusion
  1.4 0.1 copy.92
  1.5 0.1 dynamic_slice.3
  1.6 0.1 slice_bitcast_fusion.31
  1.7 0.1 iota_compare_fusion.1
  1.8 0.1 iota_compare_fusion
  1.9 2.7 %and_select_fusion = bf16[4,9,128,128]{3,2,0,1:T(8,128)(2,1)S(1)} fusion(bf16[4,9,128,128]{3,2,1,0:T(8,128)(2,1)} %param.43, pred[4,128]{1,0:T(4,128)(4,1)S(1)} %iota_compare_fusion.1, pred[4,9,128]{2,0,1:T(4,128)(4,1)S(1)} %iota_compare_fusion, pred[4,9]{0,1:T(8,128)(4,1)S(1)} %copy.92), kind=kLoop, calls=%fused_computation.6 | loop fusion | flops 1769472 | bytes 2364452 | tf_op jit(solution)/shard_map/jit(_where)/select_n | solution.py:48
  4.6 0.1 collective-permute-start
  4.6 1.7 %collective-permute-start.1 = (bf16[4,9,128,128]{3,2,0,1:T(8,128)(2,1)S(1)}, bf16[4,9,128,128]{3,2,0,1:T(8,128)(2,1)S(1)}, u32[]{:S(2)}, u32[]{:S(2)}) collective-permute-start(bf16[4,9,128,128]{3,2,0,1:T(8,128)(2,1)S(1)} %and_select_fusion), channel_id=1, source_target_pairs={{0,31},{1,0},{2,1},{3,2},{4,3},{5,4},{6,5},{7,6},{8,7},{9,8},{10,9... | collective-permute-start | bytes 3538952 | tf_op jit(solution)/shard_map/ppermute | solution.py:9
  6.4 26.5 %collective-permute-done = bf16[4,9,128,128]{3,2,0,1:T(8,128)(2,1)S(1)} collective-permute-done((bf16[4,9,128,128]{3,2,0,1:T(8,128)(2,1)S(1)}, bf16[4,9,128,128]{3,2,0,1:T(8,128)(2,1)S(1)}, u32[]{:S(2)}, u32[]{:S(2)}) %collective-permute-start) | collective-permute-done | bytes 1179680 | tf_op jit(solution)/shard_map/ppermute | solution.py:9
  32.9 0.3 fusion.15
  33.2 0.2 scatter-add.54
  33.5 0.7 add_dynamic-update-slice_fusion.1
  34.1 0.8 fusion.3
  34.9 0.9 %fusion.1 = f32[4,9,128,128]{3,2,0,1:T(8,128)S(1)} fusion(f32[4,9,128,128]{3,2,0,1:T(8,128)S(1)} %fusion.3, bf16[4,9,128,128]{3,2,0,1:T(8,128)(2,1)S(1)} %and_select_fusion, bf16[4,9,128,128]{3,2,0,1:T(8,128)(2,1)S(1)} %collective-permute-done), kind=kOutput, calls=%fused_computation.12 | convolution fusion | flops 139460608 | bytes 6684672 | tf_op jit(solution)/shard_map/jsab,jbc->jsac/dot_general | solution.py:20
  35.8 0.5 convolution_add_fusion.1
  36.2 9.1 %collective-permute-done.1 = bf16[4,9,128,128]{3,2,0,1:T(8,128)(2,1)S(1)} collective-permute-done((bf16[4,9,128,128]{3,2,0,1:T(8,128)(2,1)S(1)}, bf16[4,9,128,128]{3,2,0,1:T(8,128)(2,1)S(1)}, u32[]{:S(2)}, u32[]{:S(2)}) %collective-permute-start.1) | collective-permute-done | bytes 1179680 | tf_op jit(solution)/shard_map/ppermute | solution.py:9
  45.4 1.0 %constant_dynamic-update-slice_fusion.5 = (f32[4,9,128,128]{3,2,0,1:T(8,128)S(1)}, f32[4,8,128,128]{3,2,0,1:T(8,128)S(1)}) fusion(f32[4,9,128,128]{3,2,0,1:T(8,128)S(1)} %convolution_add_fusion.1, bf16[4,9,128,128]{3,2,0,1:T(8,128)(2,1)S(1)} %and_select_fusion, bf16[4,9,128,128]{3,2,0,1:T(8,128)(2,1)S(1)} %collective-permute-done.1), kind=kOutput, calls=%fused_computation.56 | convolution fusion | flops 139460608 | bytes 8781824 | tf_op jit(solution)/shard_map/jsab,jbc->jsac/dot_general | solution.py:20
  46.4 0.4 constant_dynamic-update-slice_fusion.4
  46.8 0.4 constant_dynamic-update-slice_fusion.3
  47.2 0.3 fusion.5
  47.5 0.3 select_convert_fusion.1
  47.8 0.1 collective-permute-start.2
  47.9 2.0 %collective-permute-start.3 = (bf16[4,9,128,128]{3,2,0,1:T(8,128)(2,1)S(1)}, bf16[4,9,128,128]{3,2,0,1:T(8,128)(2,1)S(1)}, u32[]{:S(2)}, u32[]{:S(2)}) collective-permute-start(bf16[4,9,128,128]{3,2,0,1:T(8,128)(2,1)S(1)} %select_convert_fusion.1), channel_id=1, source_target_pairs={{0,31},{1,0},{2,1},{3,2},{4,3},{5,4},{6,5},{7,6},{8,7},{9,8},{10,9... | collective-permute-start | bytes 3538952 | tf_op jit(solution)/shard_map/ppermute | solution.py:9
  49.8 26.5 %collective-permute-done.2 = bf16[4,9,128,128]{3,2,0,1:T(8,128)(2,1)S(1)} collective-permute-done((bf16[4,9,128,128]{3,2,0,1:T(8,128)(2,1)S(1)}, bf16[4,9,128,128]{3,2,0,1:T(8,128)(2,1)S(1)}, u32[]{:S(2)}, u32[]{:S(2)}) %collective-permute-start.2) | collective-permute-done | bytes 1179680 | tf_op jit(solution)/shard_map/ppermute | solution.py:9
  76.3 0.3 fusion.14
  76.6 0.2 scatter-add.66
  76.8 0.7 add_dynamic-update-slice_fusion
  77.5 0.8 fusion.2
  78.3 0.9 %fusion = f32[4,9,128,128]{3,2,0,1:T(8,128)S(1)} fusion(f32[4,9,128,128]{3,2,0,1:T(8,128)S(1)} %fusion.2, bf16[4,9,128,128]{3,2,0,1:T(8,128)(2,1)S(1)} %select_convert_fusion.1, bf16[4,9,128,128]{3,2,0,1:T(8,128)(2,1)S(1)} %collective-permute-done.2, bf16[4,9,128,128]{3,2,0,1:T(8,128)(2,1)S(1)} %and_select_fusion), kind=kOutput, calls=%fused_computation.9 | convolution fusion | flops 139460608 | bytes 6684672 | tf_op jit(solution)/shard_map/jsab,jbc->jsac/dot_general | solution.py:20
  79.2 0.5 convolution_add_fusion
  79.6 0.0 collective-permute-done.3
  79.6 1.0 %constant_dynamic-update-slice_fusion.2 = (f32[4,9,128,128]{3,2,0,1:T(8,128)S(1)}, f32[4,8,128,128]{3,2,0,1:T(8,128)S(1)}) fusion(f32[4,9,128,128]{3,2,0,1:T(8,128)S(1)} %convolution_add_fusion, bf16[4,9,128,128]{3,2,0,1:T(8,128)(2,1)S(1)} %and_select_fusion, bf16[4,9,128,128]{3,2,0,1:T(8,128)(2,1)S(1)} %collective-permute-done.3, ...), kind=kOutput, calls=%fused_computation.53 | convolution fusion | flops 139460608 | bytes 8781824 | tf_op jit(solution)/shard_map/jsab,jbc->jsac/dot_general | solution.py:20
  80.7 0.4 constant_dynamic-update-slice_fusion.1
  81.1 0.4 constant_dynamic-update-slice_fusion
  81.5 0.3 fusion.4
  81.8 0.6 select_convert_fusion
  82.4 1.1 %copy.130 = bf16[4,9,128,128]{3,2,1,0:T(8,128)(2,1)} copy(bf16[4,9,128,128]{3,2,0,1:T(8,128)(2,1)S(1)} %select_convert_fusion) | data formatting | bytes 2359296 | tf_op jit(solution)/shard_map/convert_element_type | solution.py:80
  (1 shorter events, 0.0 us)
Async XLA Ops:
  4.6 28.3 %collective-permute-start = (bf16[4,9,128,128]{3,2,0,1:T(8,128)(2,1)S(1)}, bf16[4,9,128,128]{3,2,0,1:T(8,128)(2,1)S(1)}, u32[]{:S(2)}, u32[]{:S(2)}) collective-permute-start(bf16[4,9,128,128]{3,2,0,1:T(8,128)(2,1)S(1)} %and_select_fusion), channel_id=1, source_target_pairs={{0,1},{1,2},{2,3},{3,4},{4,5},{5,6},{6,7},{7,8},{8,9},{9,10},{10,1... | collective-permute-start | bytes 3538952 | tf_op jit(solution)/shard_map/ppermute | solution.py:9
  4.6 40.7 %collective-permute-start.1 = (bf16[4,9,128,128]{3,2,0,1:T(8,128)(2,1)S(1)}, bf16[4,9,128,128]{3,2,0,1:T(8,128)(2,1)S(1)}, u32[]{:S(2)}, u32[]{:S(2)}) collective-permute-start(bf16[4,9,128,128]{3,2,0,1:T(8,128)(2,1)S(1)} %and_select_fusion), channel_id=1, source_target_pairs={{0,31},{1,0},{2,1},{3,2},{4,3},{5,4},{6,5},{7,6},{8,7},{9,8},{10,9... | collective-permute-start | bytes 3538952 | tf_op jit(solution)/shard_map/ppermute | solution.py:9
  47.8 28.5 %collective-permute-start.2 = (bf16[4,9,128,128]{3,2,0,1:T(8,128)(2,1)S(1)}, bf16[4,9,128,128]{3,2,0,1:T(8,128)(2,1)S(1)}, u32[]{:S(2)}, u32[]{:S(2)}) collective-permute-start(bf16[4,9,128,128]{3,2,0,1:T(8,128)(2,1)S(1)} %select_convert_fusion.1), channel_id=1, source_target_pairs={{0,1},{1,2},{2,3},{3,4},{4,5},{5,6},{6,7},{7,8},{8,9},{9,10},{10,1... | collective-permute-start | bytes 3538952 | tf_op jit(solution)/shard_map/ppermute | solution.py:9
  47.9 31.8 %collective-permute-start.3 = (bf16[4,9,128,128]{3,2,0,1:T(8,128)(2,1)S(1)}, bf16[4,9,128,128]{3,2,0,1:T(8,128)(2,1)S(1)}, u32[]{:S(2)}, u32[]{:S(2)}) collective-permute-start(bf16[4,9,128,128]{3,2,0,1:T(8,128)(2,1)S(1)} %select_convert_fusion.1), channel_id=1, source_target_pairs={{0,31},{1,0},{2,1},{3,2},{4,3},{5,4},{6,5},{7,6},{8,7},{9,8},{10,9... | collective-permute-start | bytes 3538952 | tf_op jit(solution)/shard_map/ppermute | solution.py:9
where the time goes:
time: 83.7 us; the launch traced here: 83.5 us
  waiting for transfers between devices  62.1 us (74%)
  matrix products  10.4 us (12%)
  other arithmetic  5.12 us (6%)
  starting transfers between devices  3.8 us (5%)
  local copies, waits for them, and re-layouts  1.92 us (2%)
    ppermute x4, waiting for transfers between devices, passed_along(): lax.ppermute(array, axis, [(i, (i + by) % count) for i in range(count)])  62.1 us
    dot_general x18, matrix products, column_terms(): jnp.einsum('jsab,jbc->jsac', widened[step_t:step_t + own_cols, first_row:...  10.4 us
    ppermute x4, starting transfers between devices, passed_along(): lax.ppermute(array, axis, [(i, (i + by) % count) for i in range(count)])  3.8 us
    select_n x1, other arithmetic, per_device(): masked = jnp.where(visible, density, jnp.zeros_like(density))  2.69 us
  transfers between devices with their start and end apart: 4, of which 3 were waited for; matrix products, arithmetic and copies ran while one was open for 8% of the time, Pallas kernels for 0%

commit v1 on v0

v1 whole, which is shorter than its diff:
```python
import functools

import jax
import jax.numpy as jnp
from jax import lax
from jax.experimental import pallas as pl
from jax.experimental.pallas import tpu as pltpu
from jax.sharding import PartitionSpec as P

AXES = ("blk", "rep")
MESH = pl.DeviceIdType.MESH
F32 = jnp.float32
BF16 = jnp.bfloat16


def dot(a, b):
    return jnp.dot(a, b, preferred_element_type=F32)


def tdot(a, b):
    return lax.dot_general(a, b, (((0,), (0,)), ((), ())), preferred_element_type=F32)


def kernel(
    orb, pat, den, out, m, near, sq, sqnear, acc, obuf, load_sem, store_sem, send_sem, recv_sem
):
    w, tile = den.shape[0], den.shape[2]
    band = den.shape[1]
    n_blocks = orb.shape[0]
    wide = w * tile
    rep = lax.axis_size(AXES[1])
    count = lax.axis_size(AXES[0]) * rep
    me = lax.axis_index(AXES[0]) * rep + lax.axis_index(AXES[1])
    right, left = lax.rem(me + 1, count), lax.rem(me + count - 1, count)
    right_id, left_id = (right // rep, right % rep), (left // rep, left % rep)

    barrier = pltpu.get_barrier_semaphore()
    for who in (left_id, right_id):
        pl.semaphore_signal(barrier, inc=1, device_id=who, device_id_type=MESH)

    def lanes(c):
        return pl.ds(c * tile, tile)

    def rows_of(c, p):
        return max(c, p * w), min(c + band, (p + 1) * w)

    def load(c, p):
        lo, hi = rows_of(c, p)
        return pltpu.make_async_copy(
            den.at[c, pl.ds(lo - c, hi - lo)], m.at[pl.ds(lo, hi - lo), :, lanes(c)], load_sem.at[c, p]
        )

    for p in (1, 0, 2):
        for c in range(w):
            load(c, p).start()

    row_ids = lax.broadcasted_iota(jnp.int32, (tile, tile), 0)
    col_ids = lax.broadcasted_iota(jnp.int32, (tile, tile), 1)
    first = me * w
    counts = [orb[lax.rem(first + i - w + n_blocks, n_blocks)] for i in range(3 * w)]

    def mask_part(p):
        for c in range(w):
            lo, hi = rows_of(c, p)
            load(c, p).wait()
            for i in range(lo, hi):
                limit = jnp.where(pat[c, i - c] == 1, counts[i], 0)
                seen = (row_ids < limit) & (col_ids < counts[w + c])
                block = m[i, :, lanes(c)].astype(F32)
                m[i, :, lanes(c)] = jnp.where(seen, block, 0.0).astype(BF16)
            for i in range(p * w, (p + 1) * w):
                if not lo <= i < hi:
                    m[i, :, lanes(c)] = jnp.zeros((tile, tile), BF16)

    def sends(phase, src, dst):
        made = []
        for a in range(w):
            for side, who in ((0, right_id), (1, left_id)):
                cut = pl.ds(a * tile, wide - a * tile)
                made.append(
                    pltpu.make_async_remote_copy(
                        src_ref=src.at[w + a, :, cut],
                        dst_ref=dst.at[side, a, :, cut],
                        send_sem=send_sem.at[phase, side, a],
                        recv_sem=recv_sem.at[phase, side, a],
                        device_id=who,
                        device_id_type=MESH,
                    )
                )
        return made

    def arrived(copies, buf, side):
        for a in range(w):
            copies[2 * a + side].wait_recv()
        for a in range(w):
            for b in range(a + 1, w):
                buf[side, b, :, lanes(a)] = buf[side, a, :, lanes(b)].T

    mask_part(1)
    pl.semaphore_wait(barrier, 2)
    first_sends = sends(0, m, near)
    for copy in first_sends:
        copy.start()
    mask_part(0)
    mask_part(2)

    def mat(ref, lo, hi, cols=slice(None)):
        got = ref[lo:hi, :, cols]
        return got.reshape((hi - lo) * tile, got.shape[-1])

    def kept(c, i, block):
        return jnp.where(jnp.broadcast_to(pat[c, i - c], block.shape) == 1, block, 0.0)

    acc[w : 2 * w] = tdot(mat(m, 0, 3 * w), mat(m, 0, 3 * w)).reshape(w, tile, wide)

    def filter_part(p):
        for c in range(w):
            lo, hi = rows_of(c, p)
            for i in range(p * w, (p + 1) * w):
                if lo <= i < hi:
                    sq[i, :, lanes(c)] = kept(c, i, acc[i, :, lanes(c)]).astype(BF16)
                else:
                    sq[i, :, lanes(c)] = jnp.zeros((tile, tile), BF16)

    filter_part(1)
    second_sends = sends(1, sq, sqnear)
    for copy in second_sends:
        copy.start()

    half = w // 2
    halves = [(h * half, (h + 1) * half) for h in range(2)]

    def own_term(part_ref, p):
        got = []
        for c0, c1 in halves:
            cols = slice(c0 * tile, c1 * tile)
            lo, hi = (c0, w) if p == 0 else (0, c1)
            got.append((lo, hi, cols, dot(mat(part_ref, p * w + lo, p * w + hi), mat(m, w, 2 * w, cols))))
        return got

    def near_term(buf, side):
        got = []
        for c0, c1 in halves:
            cols = slice(c0 * tile, c1 * tile)
            lo, hi = (c0, w) if side == 0 else (0, c1)
            base = 2 * w * side
            left_side = buf[side, lo:hi, :, lo * tile : hi * tile].reshape((hi - lo) * tile, (hi - lo) * tile)
            got.append((lo, hi, cols, dot(left_side, mat(m, base + lo, base + hi, cols))))
        return got

    def shaped(x):
        return x.reshape(x.shape[0] // tile, tile, x.shape[1])

    for p in (0, 2):
        for lo, hi, cols, value in own_term(m, p):
            acc[p * w + lo : p * w + hi, :, cols] = shaped(value)
    for side in (0, 1):
        p = 2 * side
        arrived(first_sends, near, side)
        for lo, hi, cols, value in near_term(near, side):
            acc[p * w + lo : p * w + hi, :, cols] += shaped(value)
        filter_part(p)
        for lo, hi, cols, value in own_term(sq, p):
            acc[p * w + lo : p * w + hi, :, cols] = 3.0 * acc[p * w + lo : p * w + hi, :, cols] - 2.0 * shaped(value)

    cube = tdot(mat(sq, 0, 3 * w), mat(m, 0, 3 * w)).reshape(w, tile, wide)
    acc[w : 2 * w] = 3.0 * acc[w : 2 * w] - 2.0 * cube

    def store(c, p):
        lo, hi = rows_of(c, p)
        return pltpu.make_async_copy(
            obuf.at[c, pl.ds(lo - c, hi - lo)], out.at[c, pl.ds(lo - c, hi - lo)], store_sem.at[c, p]
        )

    def finish(p):
        for c in range(w):
            lo, hi = rows_of(c, p)
            for i in range(lo, hi):
                obuf[c, i - c] = kept(c, i, acc[i, :, lanes(c)]).astype(BF16)
            store(c, p).start()

    finish(1)
    for side in (0, 1):
        p = 2 * side
        arrived(second_sends, sqnear, side)
        for lo, hi, cols, value in near_term(sqnear, side):
            acc[p * w + lo : p * w + hi, :, cols] -= 2.0 * shaped(value)
        finish(p)

    for copy in first_sends + second_sends:
        copy.wait_send()
    for p in range(3):
        for c in range(w):
            store(c, p).wait()


def per_device(density, pattern, orbitals):
    w, band, tile = density.shape[:3]
    assert band == 2 * w + 1 and w % 2 == 0
    wide = w * tile
    return pl.pallas_call(
        kernel,
        out_shape=jax.ShapeDtypeStruct(density.shape, density.dtype),
        in_specs=[
            pl.BlockSpec(memory_space=pltpu.SMEM),
            pl.BlockSpec(memory_space=pltpu.SMEM),
            pl.BlockSpec(memory_space=pl.ANY),
        ],
        out_specs=pl.BlockSpec(memory_space=pl.ANY),
        scratch_shapes=[
            pltpu.VMEM((3 * w, tile, wide), BF16),
            pltpu.VMEM((2, w, tile, wide), BF16),
            pltpu.VMEM((3 * w, tile, wide), BF16),
            pltpu.VMEM((2, w, tile, wide), BF16),
            pltpu.VMEM((3 * w, tile, wide), F32),
            pltpu.VMEM((w, band, tile, tile), BF16),
            pltpu.SemaphoreType.DMA((w, 3)),
            pltpu.SemaphoreType.DMA((w, 3)),
            pltpu.SemaphoreType.DMA((2, 2, w)),
            pltpu.SemaphoreType.DMA((2, 2, w)),
        ],
        compiler_params=pltpu.CompilerParams(collective_id=0, has_side_effects=True),
    )(orbitals, pattern, density)


def solution(mesh):
    placed = (P(AXES, None, None, None), P(AXES, None), P())
    return jax.shard_map(
        per_device, mesh=mesh, in_specs=placed, out_specs=P(AXES, None, None, None), check_vma=False
    )
```

time: 83.7 us -> 24 us (0.29)
  the two profiles are of different devices: /device:TPU:12 before, /device:TPU:1 now
where the time goes in v1:
time: 24 us; the launch traced here: 23.8 us
  Pallas kernels  21.4 us (89%)
  local copies, waits for them, and re-layouts  2.41 us (10%)
    pallas_call x1, Pallas kernels, per_device(): pl.pallas_call(kernel, out_shape=jax.ShapeDtypeStruct(density.shape, dens...  21.4 us
    unnamed x1, local copies, waits for them, and re-layouts  2.41 us

profile of v1, /device:TPU:1, one launch (start us, length us, event | category | flops | bytes accessed | tf_op | source)
XLA Modules:
  0.0 23.8 jit_solution(12005375855651698893)
XLA Ops:
  0.0 21.4 %shard_map.37 = bf16[4,9,128,128]{3,2,1,0:T(8,128)(2,1)} custom-call(s32[128]{0:T(128)} %orb.1, s32[4,9]{1,0:T(4,128)} %pat.1, bf16[4,9,128,128]{3,2,1,0:T(8,128)(2,1)} %den.1), custom_call_target="tpu_custom_call" | custom-call | tf_op jit(solution)/shard_map/pallas_call | solution.py:201
  21.4 2.4 %copy.5 = bf16[4,9,128,128]{3,2,1,0:T(8,128)(2,1)} copy(bf16[4,9,128,128]{3,2,1,0:T(8,128)(2,1)} %shard_map.37) | data formatting | bytes 2359296

commit v2 on v1

--- a/solution.py
+++ b/solution.py
@@ -22,7 +22,7 @@
 
 
 def kernel(
-    orb, pat, den, out, m, near, sq, sqnear, acc, obuf, load_sem, store_sem, send_sem, recv_sem
+    orb, pat, den, out, m, near, sq, sqnear, pack, got, acc, obuf, load_sem, store_sem, send_sem, recv_sem
 ):
     w, tile = den.shape[0], den.shape[2]
     band = den.shape[1]
@@ -72,15 +72,27 @@
                 if not lo <= i < hi:
                     m[i, :, lanes(c)] = jnp.zeros((tile, tile), BF16)
 
+    low = tile // 2
+    lane_ids = lax.broadcasted_iota(jnp.int32, (low, tile), 1)
+
+    def fill(phase, src):
+        for a in range(w):
+            pack[phase, pl.ds(a * low, low), :] = src[w + a, 0:low, lanes(a)]
+        for q in range(w // 2):
+            even = pltpu.roll(src[w + 2 * q, low:tile, lanes(2 * q)].astype(F32), low, 1)
+            odd = src[w + 2 * q + 1, low:tile, lanes(2 * q + 1)].astype(F32)
+            pack[phase, pl.ds((w + q) * low, low), :] = jnp.where(lane_ids < low, even, odd).astype(BF16)
+
     def sends(phase, src, dst):
         made = []
         for a in range(w):
             for side, who in ((0, right_id), (1, left_id)):
-                cut = pl.ds(a * tile, wide - a * tile)
+                cut = pl.ds((a + 1) * tile, wide - (a + 1) * tile)
+                last = a == w - 1
                 made.append(
                     pltpu.make_async_remote_copy(
-                        src_ref=src.at[w + a, :, cut],
-                        dst_ref=dst.at[side, a, :, cut],
+                        src_ref=pack.at[phase] if last else src.at[w + a, :, cut],
+                        dst_ref=got.at[phase, side] if last else dst.at[side, a, :, cut],
                         send_sem=send_sem.at[phase, side, a],
                         recv_sem=recv_sem.at[phase, side, a],
                         device_id=who,
@@ -90,13 +102,30 @@
         return made
 
     def arrived(copies, buf, side):
-        for a in range(w):
+        for a in range(w - 1):
             copies[2 * a + side].wait_recv()
-        for a in range(w):
+            buf[side, a, :, lanes(a)] = jnp.zeros((tile, tile), BF16)
             for b in range(a + 1, w):
                 buf[side, b, :, lanes(a)] = buf[side, a, :, lanes(b)].T
+        buf[side, w - 1, :, lanes(w - 1)] = jnp.zeros((tile, tile), BF16)
+
+    def diagonal_term(copies, phase, side):
+        copies[2 * (w - 1) + side].wait_recv()
+        made = []
+        for a in range(w):
+            top = got[phase, side, pl.ds(a * low, low), :].astype(F32)
+            corner = got[phase, side, pl.ds((w + a // 2) * low, low), :].astype(F32)
+            if a % 2 == 0:
+                corner = pltpu.roll(corner, low, 1)
+            turned = jnp.concatenate([top, jnp.zeros_like(top)], axis=0).T
+            block = jnp.concatenate([top, jnp.where(lane_ids < low, turned[low:tile], corner)], axis=0)
+            cols = slice(0, (a + 1) * tile) if side == 0 else slice(a * tile, wide)
+            row = 2 * w * side + a
+            made.append((row, cols, dot(block.astype(BF16), m[row, :, cols])))
+        return made
 
     mask_part(1)
+    fill(0, m)
     pl.semaphore_wait(barrier, 2)
     first_sends = sends(0, m, near)
     for copy in first_sends:
@@ -123,6 +152,7 @@
                     sq[i, :, lanes(c)] = jnp.zeros((tile, tile), BF16)
 
     filter_part(1)
+    fill(1, sq)
     second_sends = sends(1, sq, sqnear)
     for copy in second_sends:
         copy.start()
@@ -159,6 +189,8 @@
         arrived(first_sends, near, side)
         for lo, hi, cols, value in near_term(near, side):
             acc[p * w + lo : p * w + hi, :, cols] += shaped(value)
+        for row, cols, value in diagonal_term(first_sends, 0, side):
+            acc[row, :, cols] += value
         filter_part(p)
         for lo, hi, cols, value in own_term(sq, p):
             acc[p * w + lo : p * w + hi, :, cols] = 3.0 * acc[p * w + lo : p * w + hi, :, cols] - 2.0 * shaped(value)
@@ -185,6 +217,8 @@
         arrived(second_sends, sqnear, side)
         for lo, hi, cols, value in near_term(sqnear, side):
             acc[p * w + lo : p * w + hi, :, cols] -= 2.0 * shaped(value)
+        for row, cols, value in diagonal_term(second_sends, 1, side):
+            acc[row, :, cols] -= 2.0 * value
         finish(p)
 
     for copy in first_sends + second_sends:
@@ -192,13 +226,33 @@
     for p in range(3):
         for c in range(w):
             store(c, p).wait()
+
+
+def drain(src, dst, buf, in_sem, out_sem):
+    step = src.shape[1] // 3
+    pieces = [(c, q) for c in range(src.shape[0]) for q in range(3)]
+
+    def copies(c, q):
+        part = pl.ds(q * step, step if q < 2 else src.shape[1] - 2 * step)
+        return (
+            pltpu.make_async_copy(src.at[c, part], buf.at[c, part], in_sem.at[c, q]),
+            pltpu.make_async_copy(buf.at[c, part], dst.at[c, part], out_sem.at[c, q]),
+        )
+
+    for c, q in pieces:
+        copies(c, q)[0].start()
+    for c, q in pieces:
+        copies(c, q)[0].wait()
+        copies(c, q)[1].start()
+    for c, q in pieces:
+        copies(c, q)[1].wait()
 
 
 def per_device(density, pattern, orbitals):
     w, band, tile = density.shape[:3]
     assert band == 2 * w + 1 and w % 2 == 0
     wide = w * tile
-    return pl.pallas_call(
+    made = pl.pallas_call(
         kernel,
         out_shape=jax.ShapeDtypeStruct(density.shape, density.dtype),
         in_specs=[
@@ -212,6 +266,8 @@
             pltpu.VMEM((2, w, tile, wide), BF16),
             pltpu.VMEM((3 * w, tile, wide), BF16),
             pltpu.VMEM((2, w, tile, wide), BF16),
+            pltpu.VMEM((2, 3 * w * tile // 4, tile), BF16),
+            pltpu.VMEM((2, 2, 3 * w * tile // 4, tile), BF16),
             pltpu.VMEM((3 * w, tile, wide), F32),
             pltpu.VMEM((w, band, tile, tile), BF16),
             pltpu.SemaphoreType.DMA((w, 3)),
@@ -221,6 +277,17 @@
         ],
         compiler_params=pltpu.CompilerParams(collective_id=0, has_side_effects=True),
     )(orbitals, pattern, density)
+    return pl.pallas_call(
+        drain,
+        out_shape=jax.ShapeDtypeStruct(density.shape, density.dtype),
+        in_specs=[pl.BlockSpec(memory_space=pl.ANY)],
+        out_specs=pl.BlockSpec(memory_space=pl.ANY),
+        scratch_shapes=[
+            pltpu.VMEM(density.shape, density.dtype),
+            pltpu.SemaphoreType.DMA((w, 3)),
+            pltpu.SemaphoreType.DMA((w, 3)),
+        ],
+    )(made)
 
 
 def solution(mesh):

time: 24 us -> 22.4 us (0.933)
  local copies, waits for them, and re-layouts: 2.41 us -> 0 us
  Pallas kernels: 21.4 us -> 22.2 us
    unnamed x1 -> x0, local copies, waits for them, and re-layouts: 2.41 us -> none
    pallas_call x0 -> x1, Pallas kernels: none -> 2.19 us  [per_device(): pl.pallas_call(drain, out_shape=jax.ShapeDtypeStruct(density.shape, densi...]
    pallas_call x1, Pallas kernels: 21.4 us -> 20 us  [per_device(): pl.pallas_call(kernel, out_shape=jax.ShapeDtypeStruct(density.shape, dens...]
where the time goes in v2:
time: 22.4 us; the launch traced here: 22.2 us
  Pallas kernels  22.2 us (99%)
    pallas_call x1, Pallas kernels, per_device(): pl.pallas_call(kernel, out_shape=jax.ShapeDtypeStruct(density.shape, dens...  20 us
    pallas_call x1, Pallas kernels, per_device(): pl.pallas_call(drain, out_shape=jax.ShapeDtypeStruct(density.shape, densi...  2.19 us

profile of v2, /device:TPU:1, one launch (start us, length us, event | category | flops | bytes accessed | tf_op | source)
XLA Modules:
  0.0 22.2 jit_solution(5648988957902296055)
XLA Ops:
  0.0 20.0 %shard_map.37.src = bf16[4,9,128,128]{3,2,1,0:T(8,128)(2,1)} custom-call(s32[128]{0:T(128)} %orb.1, s32[4,9]{1,0:T(4,128)} %pat.1, bf16[4,9,128,128]{3,2,1,0:T(8,128)(2,1)} %den.1), custom_call_target="tpu_custom_call" | custom-call | tf_op jit(solution)/shard_map/pallas_call | solution.py:255
  20.0 2.2 %shard_map.38 = bf16[4,9,128,128]{3,2,1,0:T(8,128)(2,1)} custom-call(bf16[4,9,128,128]{3,2,1,0:T(8,128)(2,1)} %shard_map.37.src), custom_call_target="tpu_custom_call" | custom-call | tf_op jit(solution)/shard_map/pallas_call | solution.py:280

commit v3 on v2

--- a/solution.py
+++ b/solution.py
@@ -22,11 +22,14 @@
 
 
 def kernel(
-    orb, pat, den, out, m, near, sq, sqnear, pack, got, acc, obuf, load_sem, store_sem, send_sem, recv_sem
+    orb_in, pat_in, den, out, orb, pat, m, near, sq, sqnear, pack, got, acc, small_sem, load_sem, send_sem, recv_sem
 ):
     w, tile = den.shape[0], den.shape[2]
     band = den.shape[1]
     n_blocks = orb.shape[0]
+    small = [pltpu.make_async_copy(orb_in, orb, small_sem.at[0]), pltpu.make_async_copy(pat_in, pat, small_sem.at[1])]
+    for copy in small:
+        copy.start()
     wide = w * tile
     rep = lax.axis_size(AXES[1])
     count = lax.axis_size(AXES[0]) * rep
@@ -57,6 +60,8 @@
     row_ids = lax.broadcasted_iota(jnp.int32, (tile, tile), 0)
     col_ids = lax.broadcasted_iota(jnp.int32, (tile, tile), 1)
     first = me * w
+    for copy in small:
+        copy.wait()
     counts = [orb[lax.rem(first + i - w + n_blocks, n_blocks)] for i in range(3 * w)]
 
     def mask_part(p):
@@ -125,10 +130,12 @@
         return made
 
     mask_part(1)
-    fill(0, m)
     pl.semaphore_wait(barrier, 2)
     first_sends = sends(0, m, near)
-    for copy in first_sends:
+    for copy in first_sends[:-2]:
+        copy.start()
+    fill(0, m)
+    for copy in first_sends[-2:]:
         copy.start()
     mask_part(0)
     mask_part(2)
@@ -198,18 +205,11 @@
     cube = tdot(mat(sq, 0, 3 * w), mat(m, 0, 3 * w)).reshape(w, tile, wide)
     acc[w : 2 * w] = 3.0 * acc[w : 2 * w] - 2.0 * cube
 
-    def store(c, p):
-        lo, hi = rows_of(c, p)
-        return pltpu.make_async_copy(
-            obuf.at[c, pl.ds(lo - c, hi - lo)], out.at[c, pl.ds(lo - c, hi - lo)], store_sem.at[c, p]
-        )
-
     def finish(p):
         for c in range(w):
             lo, hi = rows_of(c, p)
             for i in range(lo, hi):
-                obuf[c, i - c] = kept(c, i, acc[i, :, lanes(c)]).astype(BF16)
-            store(c, p).start()
+                out[c, i - c] = kept(c, i, acc[i, :, lanes(c)]).astype(BF16)
 
     finish(1)
     for side in (0, 1):
@@ -223,29 +223,14 @@
 
     for copy in first_sends + second_sends:
         copy.wait_send()
-    for p in range(3):
-        for c in range(w):
-            store(c, p).wait()
-
-
-def drain(src, dst, buf, in_sem, out_sem):
-    step = src.shape[1] // 3
-    pieces = [(c, q) for c in range(src.shape[0]) for q in range(3)]
-
-    def copies(c, q):
-        part = pl.ds(q * step, step if q < 2 else src.shape[1] - 2 * step)
-        return (
-            pltpu.make_async_copy(src.at[c, part], buf.at[c, part], in_sem.at[c, q]),
-            pltpu.make_async_copy(buf.at[c, part], dst.at[c, part], out_sem.at[c, q]),
-        )
-
-    for c, q in pieces:
-        copies(c, q)[0].start()
-    for c, q in pieces:
-        copies(c, q)[0].wait()
-        copies(c, q)[1].start()
-    for c, q in pieces:
-        copies(c, q)[1].wait()
+
+
+def drain(src, dst, sem):
+    copies = [pltpu.make_async_copy(src.at[c], dst.at[c], sem.at[c]) for c in range(src.shape[0])]
+    for copy in copies:
+        copy.start()
+    for copy in copies:
+        copy.wait()
 
 
 def per_device(density, pattern, orbitals):
@@ -256,12 +241,14 @@
         kernel,
         out_shape=jax.ShapeDtypeStruct(density.shape, density.dtype),
         in_specs=[
-            pl.BlockSpec(memory_space=pltpu.SMEM),
-            pl.BlockSpec(memory_space=pltpu.SMEM),
-            pl.BlockSpec(memory_space=pl.ANY),
+            pl.BlockSpec(memory_space=pltpu.HBM),
+            pl.BlockSpec(memory_space=pltpu.HBM),
+            pl.BlockSpec(memory_space=pltpu.HBM),
         ],
-        out_specs=pl.BlockSpec(memory_space=pl.ANY),
+        out_specs=pl.BlockSpec(memory_space=pltpu.VMEM),
         scratch_shapes=[
+            pltpu.SMEM(orbitals.shape, orbitals.dtype),
+            pltpu.SMEM(pattern.shape, pattern.dtype),
             pltpu.VMEM((3 * w, tile, wide), BF16),
             pltpu.VMEM((2, w, tile, wide), BF16),
             pltpu.VMEM((3 * w, tile, wide), BF16),
@@ -269,24 +256,20 @@
             pltpu.VMEM((2, 3 * w * tile // 4, tile), BF16),
             pltpu.VMEM((2, 2, 3 * w * tile // 4, tile), BF16),
             pltpu.VMEM((3 * w, tile, wide), F32),
-            pltpu.VMEM((w, band, tile, tile), BF16),
-            pltpu.SemaphoreType.DMA((w, 3)),
+            pltpu.SemaphoreType.DMA((2,)),
             pltpu.SemaphoreType.DMA((w, 3)),
             pltpu.SemaphoreType.DMA((2, 2, w)),
             pltpu.SemaphoreType.DMA((2, 2, w)),
         ],
-        compiler_params=pltpu.CompilerParams(collective_id=0, has_side_effects=True),
-    )(orbitals, pattern, density)
+        compiler_params=pltpu.CompilerParams(collective_id=0, has_side_effects=True, vmem_limit_bytes=24 << 20),
+    )(*(pltpu.with_memory_space_constraint(x, pltpu.HBM) for x in (orbitals, pattern, density)))
     return pl.pallas_call(
         drain,
         out_shape=jax.ShapeDtypeStruct(density.shape, density.dtype),
-        in_specs=[pl.BlockSpec(memory_space=pl.ANY)],
+        in_specs=[pl.BlockSpec(memory_space=pltpu.VMEM)],
         out_specs=pl.BlockSpec(memory_space=pl.ANY),
-        scratch_shapes=[
-            pltpu.VMEM(density.shape, density.dtype),
-            pltpu.SemaphoreType.DMA((w, 3)),
-            pltpu.SemaphoreType.DMA((w, 3)),
-        ],
+        scratch_shapes=[pltpu.SemaphoreType.DMA((w,))],
+        compiler_params=pltpu.CompilerParams(vmem_limit_bytes=4 << 20),
     )(made)
 
 

time: 22.4 us -> 19.7 us (0.88)
  Pallas kernels: 22.2 us -> 19.5 us
    pallas_call x1, Pallas kernels: 20 us -> 18.5 us  [per_device(): pl.pallas_call(kernel, out_shape=jax.ShapeDtypeStruct(density.shape, dens...]
    pallas_call x1, Pallas kernels: 2.19 us -> 1.04 us  [per_device(): pl.pallas_call(drain, out_shape=jax.ShapeDtypeStruct(density.shape, densi...]
where the time goes in v3:
time: 19.7 us; the launch traced here: 19.5 us
  Pallas kernels  19.5 us (99%)
    pallas_call x1, Pallas kernels, per_device(): pl.pallas_call(kernel, out_shape=jax.ShapeDtypeStruct(density.shape, dens...  18.5 us
    pallas_call x1, Pallas kernels, per_device(): pl.pallas_call(drain, out_shape=jax.ShapeDtypeStruct(density.shape, densi...  1.04 us

profile of v3, /device:TPU:1, one launch (start us, length us, event | category | flops | bytes accessed | tf_op | source)
XLA Modules:
  0.0 19.5 jit_solution(9702589773521468437)
XLA Ops:
  0.0 18.5 %shard_map.37.src = bf16[4,9,128,128]{3,2,1,0:T(8,128)(2,1)S(1)} custom-call(s32[128]{0:T(128)} %orb_in.1, s32[4,9]{1,0:T(4,128)} %pat_in.1, bf16[4,9,128,128]{3,2,1,0:T(8,128)(2,1)} %den.1), custom_call_target="tpu_custom_call" | custom-call | tf_op jit(solution)/shard_map/pallas_call | solution.py:240
  18.5 1.0 %shard_map.38 = bf16[4,9,128,128]{3,2,1,0:T(8,128)(2,1)} custom-call(bf16[4,9,128,128]{3,2,1,0:T(8,128)(2,1)S(1)} %shard_map.37.src), custom_call_target="tpu_custom_call" | custom-call | tf_op jit(solution)/shard_map/pallas_call | solution.py:266
